TPU v7x, 128 devices: a whole 4x4x4 slice. The times are simulated.
128 devices in a mesh: sec: 2 (over x_lo), batch: 32 (over z, y, core), head: 2 (over x_hi).
Axes of the slice: x: 4 (x_hi: 2, x_lo: 2; x = x_hi * 2 + x_lo), y: 4, z: 4, core: 2. Of those that a mesh axis runs over, the one named last changes fastest.
Arguments:
- hidden_in: bfloat16 [1024, 7168], P('batch'), may hold values from -6 to 6
- queries: bfloat16 [1024, 128, 576], P('batch', ('sec', 'head')), may hold values from -8 to 8
- latent_cache: bfloat16 [1024, 192, 576], P('batch'), may hold values from -8 to 8
- new_latent: bfloat16 [1024, 576], P('batch'), may hold values from -8 to 8
- cache_lengths: int32 [1024], P('batch'), may hold values from 1 to 192, 98304 in all
- value_up: bfloat16 [128, 512, 128], P(('sec', 'head')), may hold values from -0.25 to 0.25
- out_proj: bfloat16 [16384, 7168], P(('sec', 'head'), 'batch'), may hold values from -0.046875 to 0.046875
- norm_gain: float32 [7168], replicated, may hold values from 0.1 to 1.9
- router: bfloat16 [7168, 32], replicated, may hold values from -0.03125 to 0.03125
- expert_ids: int32 [1024, 8], P('batch'), may hold values from 0 to 31, all different within a row; in each aligned block of 32 rows (0 to 31, 32 to 63, ...) at most 16 rows name the same one
- w_gate_up: bfloat16 [32, 7168, 2, 1024], P('batch', None, None, ('sec', 'head')), may hold values from -0.0625 to 0.0625
- w_down: bfloat16 [32, 1024, 7168], P('batch', ('sec', 'head')), may hold values from -0.1875 to 0.1875
Outputs:
- mixed_out: bfloat16 [1024, 7168], P('batch', ('sec', 'head'))
Inputs may be any that keep to these rules, and one draw needn't show every extreme that they name: `expert_ids`: each row names 8 different experts. Among the 32 rows of one index of batch (aligned blocks) no expert is named by more than 16 rows, a bound that some block reaches. `cache_lengths`: the lengths of all rows add up to 98304, and one row has exactly 192.
All inputs are finite; a program needn't handle non-finite values. No bound on the sum of `cache_lengths` on one device may be relied on, other than what follows from the above.
Results may differ from a plain program's by a relative error of at most 0.007.
Values may be sent and summed in bfloat16 or wider, within the bound.
A program may use at most 128 MiB of HBM per device.

v0:
```python
import jax
import jax.numpy as jnp
from jax import lax
from jax.sharding import PartitionSpec as P

QKD = 192
TOP = 8
norm_epsilon = 1e-06
route_scale = 2.5


def body(
    hidden_in,
    queries,
    latent_cache,
    new_latent,
    cache_lengths,
    value_up,
    out_proj,
    norm_gain,
    router,
    expert_ids,
    w_gate_up,
    w_down,
):
    row_count = hidden_in.shape[0]
    model_width = hidden_in.shape[1]
    latent_width = value_up.shape[1]
    cache_depth = latent_cache.shape[1]
    group_count = lax.axis_size("batch")
    slice_count = lax.axis_size(("sec", "head"))
    slice_index = lax.axis_index(("sec", "head"))
    column_width = model_width // slice_count
    capacity = min(row_count, 2 * row_count * TOP // group_count)
    score_scale = QKD ** (-0.5)
    scores = (
        jnp.einsum("thk,tjk->thj", queries, latent_cache, preferred_element_type=jnp.float32)
        * score_scale
    )
    own_score = (
        jnp.einsum("thk,tk->th", queries, new_latent, preferred_element_type=jnp.float32)
        * score_scale
    )
    positions = lax.broadcasted_iota(jnp.int32, (1, 1, cache_depth), 2)
    in_cache = positions < cache_lengths[:, None, None]
    scores = jnp.where(in_cache, scores, -jnp.inf)
    top_score = jnp.maximum(jnp.max(scores, axis=2), own_score)
    cache_exp = jnp.exp(scores - top_score[:, :, None])
    own_exp = jnp.exp(own_score - top_score)
    softmax_sum = jnp.sum(cache_exp, axis=2) + own_exp
    cache_weights = (cache_exp / softmax_sum[:, :, None]).astype(jnp.bfloat16)
    own_weights = (own_exp / softmax_sum).astype(jnp.bfloat16)
    latent_out = jnp.einsum(
        "thj,tjc->thc",
        cache_weights,
        latent_cache[:, :, :latent_width],
        preferred_element_type=jnp.float32,
    )
    latent_out = latent_out + own_weights.astype(jnp.float32)[:, :, None] * new_latent[
        :, None, :latent_width
    ].astype(jnp.float32)
    latent_out = latent_out.astype(jnp.bfloat16)
    head_out = jnp.einsum(
        "thc,hcd->thd", latent_out, value_up, preferred_element_type=jnp.float32
    ).astype(jnp.bfloat16)
    head_out = head_out.reshape(row_count, -1)
    column_part = jnp.dot(
        lax.all_gather(head_out, "batch", axis=0, tiled=True),
        out_proj,
        preferred_element_type=jnp.float32,
    )
    row_part = lax.all_to_all(column_part, "batch", split_axis=0, concat_axis=1, tiled=True)
    attention = lax.psum(row_part, ("sec", "head"))
    residual = hidden_in.astype(jnp.float32) + attention
    mean_square = jnp.mean(residual * residual, axis=1, keepdims=True)
    normed = (residual * lax.rsqrt(mean_square + norm_epsilon) * norm_gain).astype(jnp.bfloat16)
    logits = jnp.dot(normed, router, preferred_element_type=jnp.float32)
    affinity = jax.nn.sigmoid(logits)
    expert_grid = lax.broadcasted_iota(jnp.int32, (1, 1, group_count), 2)
    hit_table = expert_ids[:, :, None] == expert_grid
    picked = jnp.sum(jnp.where(hit_table, affinity[:, None, :], 0.0), axis=2)
    route_weights = route_scale * picked / jnp.sum(picked, axis=1, keepdims=True)
    flat_hits = hit_table.reshape(row_count * TOP, group_count).astype(jnp.int32)
    earlier = jnp.cumsum(flat_hits, axis=0) - flat_hits
    slot_index = jnp.sum(earlier * flat_hits, axis=1)
    position = expert_ids.reshape(-1) * capacity + slot_index
    buffer_grid = lax.broadcasted_iota(jnp.int32, (1, group_count * capacity), 1)
    place_table = (position[:, None] == buffer_grid).astype(jnp.bfloat16)
    dispatch_table = jnp.sum(place_table.reshape(row_count, TOP, group_count * capacity), axis=1)
    gate_up_weight = w_gate_up[0].reshape(model_width, -1)
    hidden_share = w_down.shape[1]
    outgoing = jnp.einsum("rs,rd->sd", dispatch_table, normed, preferred_element_type=jnp.float32)
    outgoing = outgoing.astype(jnp.bfloat16).reshape(group_count, capacity, model_width)
    arrived = lax.all_to_all(outgoing, "batch", split_axis=0, concat_axis=0, tiled=True)
    flat_in = arrived.reshape(-1, model_width)
    gate_up = jnp.dot(flat_in, gate_up_weight, preferred_element_type=jnp.float32)
    activated = (jax.nn.silu(gate_up[:, :hidden_share]) * gate_up[:, hidden_share:]).astype(
        jnp.bfloat16
    )
    result = jnp.dot(activated, w_down[0], preferred_element_type=jnp.float32)
    partial_out = result.reshape(arrived.shape[0], arrived.shape[1], model_width)
    summed_out = lax.psum_scatter(partial_out, ("sec", "head"), scatter_dimension=2, tiled=True)
    returned = lax.all_to_all(summed_out, "batch", split_axis=0, concat_axis=0, tiled=True)
    flat_back = returned.reshape(group_count * capacity, column_width)
    gathered = flat_back[position].reshape(row_count, TOP, column_width)
    mixture = jnp.sum(gathered * route_weights[:, :, None], axis=1)
    residual_cols = lax.dynamic_slice_in_dim(residual, slice_index * column_width, column_width, 1)
    return (residual_cols + mixture).astype(jnp.bfloat16)


def solution(mesh):
    in_specs = (
        P("batch", None),
        P("batch", ("sec", "head"), None),
        P("batch", None, None),
        P("batch", None),
        P("batch"),
        P(("sec", "head"), None, None),
        P(("sec", "head"), "batch"),
        P(),
        P(),
        P("batch", None),
        P("batch", None, None, ("sec", "head")),
        P("batch", ("sec", "head"), None),
    )
    out_specs = P("batch", ("sec", "head"))
    return jax.shard_map(body, mesh=mesh, in_specs=in_specs, out_specs=out_specs, check_vma=False)
```

profile of v0, /device:TPU:0, one launch (start us, length us, event | category | flops | bytes accessed | tf_op | source)
XLA Modules:
  0.0 588.6 jit_solution(7912476928784417901)
XLA Ops:
  6.5 0.9 iota_compare_fusion.4
  7.4 0.8 slice_convert_fusion
  8.2 1.8 fusion.19
  10.0 6.8 %fusion.28 = (f32[32,32]{1,0:T(8,128)S(1)}, f32[32,32,192]{2,1,0:T(8,128)S(1)}) fusion(bf16[32,32,576]{2,1,0:T(8,128)(2,1)} %param.13, bf16[32,192,576]{2,1,0:T(8,128)(2,1)} %param.14, pred[32,192]{1,0:T(8,128)(4,1)S(1)} %iota_compare_fusion.4), kind=kOutput, calls=%fused_computation.60 | convolution fusion | flops 227081216 | bytes 9054208 | tf_op jit(solution)/shard_map/thk,tjk->thj/dot_general | solution.py:37
  17.2 1.5 add_convert_fusion
  19.4 1.1 fusion.8
  20.5 0.8 copy.55
  21.3 55.6 %all-gather.2.cloned.1.call-done = bf16[1024,4096]{1,0:T(8,128)(2,1)} async-done(((bf16[32,4096]{1,0:T(8,128)(2,1)}), bf16[1024,4096]{1,0:T(8,128)(2,1)}) %all-gather.2.cloned.1.call-update) | async-done | bytes 8388624 | tf_op jit(solution)/shard_map/all_gather | solution.py:68
  76.9 5.7 fusion.29
  82.7 22.8 %all_to_all.29 = f32[32,32,224]{2,1,0:T(8,128)S(1)} all-to-all(f32[32,32,224]{2,1,0:T(8,128)S(1)} %bitcast.63), channel_id=1, replica_groups=mesh['sec'=2,'batch'=32,'head'=2] {'batch'}, dimensions={0} | all-to-all | bytes 1835008 | tf_op jit(solution)/shard_map/all_to_all | solution.py:72
  106.0 1.6 all_to_all.23
  109.2 41.3 %all-reduce.2.cloned.1.call-done = f32[32,7168]{1,0:T(8,128)} async-done(((f32[32,7168]{1,0:T(8,128)}), f32[32,7168]{1,0:T(8,128)}) %all-reduce.2.cloned.1.call-update) | async-done | bytes 917520 | tf_op jit(solution)/shard_map/psum | solution.py:73
  150.5 1.4 multiply_reduce_fusion
  151.9 5.1 convolution_convert_fusion
  157.1 7.4 %all-to-all-start.1 = ((bf16[32,16,7168]{2,1,0:T(8,128)(2,1)}), bf16[32,16,7168]{2,1,0:T(8,128)(2,1)}, u32[]{:S(2)}, u32[]{:S(2)}) async-start(bf16[32,16,7168]{2,1,0:T(8,128)(2,1)} %bitcast.58), calls=%async_computation.1 | async-start | bytes 14680064 | tf_op jit(solution)/shard_map/all_to_all | solution.py:94
  164.7 7.3 %copy.48 = bf16[896,8,2,256]{3,1,2,0:T(8,128)(2,1)} copy(bf16[896,8,2,256]{3,2,1,0:T(2,128)(2,1)} %bitcast.59) | data formatting | bytes 14680064
  172.0 84.8 %all-to-all-done.1 = bf16[32,16,7168]{2,1,0:T(8,128)(2,1)} async-done(((bf16[32,16,7168]{2,1,0:T(8,128)(2,1)}), bf16[32,16,7168]{2,1,0:T(8,128)(2,1)}, u32[]{:S(2)}, u32[]{:S(2)}) %all-to-all-start.1) | async-done | bytes 7340064 | tf_op jit(solution)/shard_map/all_to_all | solution.py:94
  256.8 8.6 %fusion.30 = f32[512,512]{1,0:T(8,128)S(1)} fusion(bf16[512,7168]{1,0:T(8,128)(2,1)} %bitcast.8, bf16[7168,512]{1,0:T(8,128)(2,1)} %bitcast.60), kind=kOutput, calls=%fused_computation.62 | convolution fusion | flops 3758096384 | bytes 15728640 | tf_op jit(solution)/shard_map/dot_general | solution.py:96
  265.5 7.3 %fusion.2 = f32[32,16,7168]{2,1,0:T(8,128)} fusion(bf16[32,16,256]{2,1,0:T(8,128)(2,1)S(1)} %bitcast.62, bf16[1,256,7168]{2,1,0:T(8,128)(2,1)S(1)} %copy-done.4), kind=kOutput, calls=%fused_computation.4 | convolution fusion | flops 1879048192 | bytes 18612224 | tf_op jit(solution)/shard_map/dot_general | solution.py:100
  272.9 245.9 %reduce-scatter.2.cloned.1.call-done = f32[32,16,1792]{2,1,0:T(8,128)} async-done(((f32[32,16,7168]{2,1,0:T(8,128)}), f32[32,16,1792]{2,1,0:T(8,128)}) %reduce-scatter.2.cloned.1.call-update) | async-done | bytes 3670032 | tf_op jit(solution)/shard_map/reduce_scatter | solution.py:102
  518.7 7.4 %all-to-all-start.2 = ((f32[32,16,1792]{2,1,0:T(8,128)}), f32[32,16,1792]{2,1,0:T(8,128)}, u32[]{:S(2)}, u32[]{:S(2)}) async-start(f32[32,16,1792]{2,1,0:T(8,128)} %reduce-scatter.2.cloned.1.call-done), calls=%async_computation.3 | async-start | bytes 7340032 | tf_op jit(solution)/shard_map/all_to_all | solution.py:103
  527.2 46.6 %all-to-all-done.2 = f32[32,16,1792]{2,1,0:T(8,128)} async-done(((f32[32,16,1792]{2,1,0:T(8,128)}), f32[32,16,1792]{2,1,0:T(8,128)}, u32[]{:S(2)}, u32[]{:S(2)}) %all-to-all-start.2) | async-done | bytes 3670048 | tf_op jit(solution)/shard_map/all_to_all | solution.py:103
  573.8 5.5 gather_fusion
  579.3 2.1 fusion.4
  (49 shorter events, 5.4 us)
Async XLA Ops:
  6.5 70.3 %copy-start = (bf16[4096,224]{0,1:T(8,128)(2,1)S(1)}, bf16[4096,224]{0,1:T(8,128)(2,1)}, u32[]{:S(2)}) copy-start(bf16[4096,224]{0,1:T(8,128)(2,1)} %param.18) | copy-start | bytes 5505028
  6.5 70.3 %all-gather.2.cloned.1.call-start = ((), (), s32[]{:S(2)}) async-start(), calls=%async_computation.4 | async-start | bytes 8650752 | tf_op jit(solution)/shard_map/all_gather | solution.py:68
  10.0 7.2 %copy-start.2 = (bf16[32,192,576]{2,1,0:T(8,128)(2,1)S(1)}, bf16[32,192,576]{2,1,0:T(8,128)(2,1)}, u32[]{:S(2)}) copy-start(bf16[32,192,576]{2,1,0:T(8,128)(2,1)} %param.14) | copy-start | bytes 21233668
  17.2 2.2 copy-start.3
  21.2 129.3 %all-reduce.2.cloned.1.call-start = ((), (), s32[]{:S(2)}) async-start(), calls=%async_computation.5 | async-start | bytes 1835008 | tf_op jit(solution)/shard_map/psum | solution.py:73
  82.6 25.0 %copy-start.8 = (s32[32,8]{0,1:T(8,128)S(1)}, s32[32,8]{0,1:T(8,128)}, u32[]{:S(2)}) copy-start(s32[32,8]{0,1:T(8,128)} %param.21) | copy-start | bytes 3076
  82.6 67.9 %copy-start.5 = (bf16[32,7168]{1,0:T(8,128)(2,1)S(1)}, bf16[32,7168]{1,0:T(8,128)(2,1)}, u32[]{:S(2)}) copy-start(bf16[32,7168]{1,0:T(8,128)(2,1)} %param.12) | copy-start | bytes 1376260
  105.4 46.5 %copy-start.7 = (f32[7168]{0:T(1024)S(1)}, f32[7168]{0:T(1024)}, u32[]{:S(2)}) copy-start(f32[7168]{0:T(1024)} %param.19) | copy-start | bytes 86020
  157.1 99.7 %all-to-all-start.1 = ((bf16[32,16,7168]{2,1,0:T(8,128)(2,1)}), bf16[32,16,7168]{2,1,0:T(8,128)(2,1)}, u32[]{:S(2)}, u32[]{:S(2)}) async-start(bf16[32,16,7168]{2,1,0:T(8,128)(2,1)} %bitcast.58), calls=%async_computation.1 | async-start | bytes 14680064 | tf_op jit(solution)/shard_map/all_to_all | solution.py:94
  164.5 354.3 %reduce-scatter.2.cloned.1.call-start = ((), (), s32[]{:S(2)}) async-start(), calls=%async_computation.6 | async-start | bytes 18350080 | tf_op jit(solution)/shard_map/reduce_scatter | solution.py:102
  256.8 8.8 %copy-start.4 = (bf16[1,256,7168]{2,1,0:T(8,128)(2,1)S(1)}, bf16[1,256,7168]{2,1,0:T(8,128)(2,1)}, u32[]{:S(2)}) copy-start(bf16[1,256,7168]{2,1,0:T(8,128)(2,1)} %param.23) | copy-start | bytes 11010052
  272.8 253.4 %copy-start.6 = (bf16[7168,32]{0,1:T(8,128)(2,1)S(1)}, bf16[7168,32]{0,1:T(8,128)(2,1)}, u32[]{:S(2)}) copy-start(bf16[7168,32]{0,1:T(8,128)(2,1)} %param.20) | copy-start | bytes 1376260
  518.7 55.1 %all-to-all-start.2 = ((f32[32,16,1792]{2,1,0:T(8,128)}), f32[32,16,1792]{2,1,0:T(8,128)}, u32[]{:S(2)}, u32[]{:S(2)}) async-start(f32[32,16,1792]{2,1,0:T(8,128)} %reduce-scatter.2.cloned.1.call-done), calls=%async_computation.3 | async-start | bytes 7340032 | tf_op jit(solution)/shard_map/all_to_all | solution.py:103
  573.8 8.3 %copy-start.1 = (bf16[4096,224]{0,1:T(8,128)(2,1)S(1)}, bf16[4096,224]{0,1:T(8,128)(2,1)}, u32[]{:S(2)}) copy-start(bf16[4096,224]{0,1:T(8,128)(2,1)} %param.18) | copy-start | bytes 5505028
Sparse Core Ops, SparseCore 0:
  21.4 55.4 all-gather.1
  107.8 42.6 all-reduce.1
  273.0 245.7 reduce-scatter.1
where the time goes:
time: 589 us
  waiting for transfers between devices  474 us (80%)
  matrix products  38.3 us (7%)
  blocking collectives  22.8 us (4%)
  local copies, waits for them, and re-layouts  17.1 us (3%)
  starting transfers between devices  15 us (3%)
  between operations  13.3 us (2%)
  other arithmetic  7.99 us (1%)
    reduce_scatter x1, waiting for transfers between devices, body(): lax.psum_scatter(partial_out, ('sec', 'head'), scatter_dimension=2, tiled...  246 us
    all_to_all x1, waiting for transfers between devices, body(): lax.all_to_all(outgoing, 'batch', split_axis=0, concat_axis=0, tiled=True)  84.8 us
    all_gather x1, waiting for transfers between devices, body(): lax.all_gather(head_out, 'batch', axis=0, tiled=True)  55.6 us
    all_to_all x1, waiting for transfers between devices, body(): lax.all_to_all(summed_out, 'batch', split_axis=0, concat_axis=0, tiled=True)  46.6 us
    psum x1, waiting for transfers between devices, body(): attention = lax.psum(row_part, ('sec', 'head'))  41.3 us
    all_to_all x1, blocking collectives, body(): lax.all_to_all(column_part, 'batch', split_axis=0, concat_axis=1, tiled=T...  22.8 us
  transfers between devices with their start and end apart: 5, of which 5 were waited for; matrix products, arithmetic and copies ran while one was open for 2% of the time, Pallas kernels for 0%

commit v1 on v0

--- a/solution.py
+++ b/solution.py
@@ -65,7 +65,9 @@
     ).astype(jnp.bfloat16)
     head_out = head_out.reshape(row_count, -1)
     column_part = jnp.dot(
-        lax.all_gather(head_out, "batch", axis=0, tiled=True),
+        jnp.concatenate(
+            lax.all_to_all(jnp.stack([head_out] * lax.axis_size("batch")), "batch", 0, 0), axis=0
+        ),
         out_proj,
         preferred_element_type=jnp.float32,
     )

time: 589 us -> 634 us (1.076)
  blocking collectives: 22.8 us -> 126 us
  waiting for transfers between devices: 474 us -> 419 us
    all_to_all x0 -> x1, blocking collectives: none -> 104 us  [body(): lax.all_to_all(jnp.stack([head_out] * lax.axis_size('batch')), 'batch', 0...]
    all_gather x1 -> x0, waiting for transfers between devices: 55.6 us -> none  [body(): lax.all_gather(head_out, 'batch', axis=0, tiled=True)]
  transfers between devices with their start and end apart: 5 -> 4, of which waited for: 5 -> 4; matrix products, arithmetic and copies ran while one was open for 2% -> 2% of each run, Pallas kernels for 0% -> 0%
where the time goes in v1:
time: 634 us
  waiting for transfers between devices  419 us (66%)
  blocking collectives  126 us (20%)
  matrix products  34.9 us (6%)
  local copies, waits for them, and re-layouts  17.4 us (3%)
  starting transfers between devices  14.8 us (2%)
  between operations  13.7 us (2%)
  other arithmetic  7.98 us (1%)
    reduce_scatter x1, waiting for transfers between devices, body(): lax.psum_scatter(partial_out, ('sec', 'head'), scatter_dimension=2, tiled...  246 us
    all_to_all x1, blocking collectives, body(): lax.all_to_all(jnp.stack([head_out] * lax.axis_size('batch')), 'batch', 0...  104 us
    all_to_all x1, waiting for transfers between devices, body(): lax.all_to_all(outgoing, 'batch', split_axis=0, concat_axis=0, tiled=True)  84.9 us
    all_to_all x1, waiting for transfers between devices, body(): lax.all_to_all(summed_out, 'batch', split_axis=0, concat_axis=0, tiled=True)  46.6 us
    psum x1, waiting for transfers between devices, body(): attention = lax.psum(row_part, ('sec', 'head'))  41.3 us
    all_to_all x1, blocking collectives, body(): lax.all_to_all(column_part, 'batch', split_axis=0, concat_axis=1, tiled=T...  22 us
  transfers between devices with their start and end apart: 4, of which 4 were waited for; matrix products, arithmetic and copies ran while one was open for 2% of the time, Pallas kernels for 0%

profile of v1, /device:TPU:0, one launch (start us, length us, event | category | flops | bytes accessed | tf_op | source)
XLA Modules:
  0.0 633.7 jit_solution(2844391811962701340)
XLA Ops:
  6.5 0.9 iota_compare_fusion.4
  7.4 0.8 slice_convert_fusion
  8.2 1.8 fusion.21
  10.0 6.8 %fusion.30 = (f32[32,32]{1,0:T(8,128)S(1)}, f32[32,32,192]{2,1,0:T(8,128)S(1)}) fusion(bf16[32,32,576]{2,1,0:T(8,128)(2,1)} %param.13, bf16[32,192,576]{2,1,0:T(8,128)(2,1)} %param.14, pred[32,192]{1,0:T(8,128)(4,1)S(1)} %iota_compare_fusion.4), kind=kOutput, calls=%fused_computation.62 | convolution fusion | flops 227081216 | bytes 9054208 | tf_op jit(solution)/shard_map/thk,tjk->thj/dot_general | solution.py:37
  17.2 1.5 add_convert_fusion
  19.4 1.1 fusion.10
  20.5 1.0 stack.3
  21.6 104.2 %all_to_all.31 = bf16[32,32,4096]{2,1,0:T(8,128)(2,1)S(1)} all-to-all(bf16[32,32,4096]{2,1,0:T(8,128)(2,1)S(1)} %stack.3), channel_id=1, replica_groups=mesh['sec'=2,'batch'=32,'head'=2] {'batch'}, dimensions={0} | all-to-all | bytes 16777216 | tf_op jit(solution)/shard_map/all_to_all | solution.py:69
  125.8 2.4 fusion.5
  128.1 22.0 %all_to_all.32 = f32[32,32,224]{2,1,0:T(8,128)S(1)} all-to-all(f32[32,32,224]{2,1,0:T(8,128)S(1)} %fusion.5), channel_id=1, replica_groups=mesh['sec'=2,'batch'=32,'head'=2] {'batch'}, dimensions={0} | all-to-all | bytes 1835008 | tf_op jit(solution)/shard_map/all_to_all | solution.py:74
  150.8 1.6 all_to_all.24
  154.0 41.3 %all-reduce.2.cloned.1.call-done = f32[32,7168]{1,0:T(8,128)} async-done(((f32[32,7168]{1,0:T(8,128)}), f32[32,7168]{1,0:T(8,128)}) %all-reduce.2.cloned.1.call-update) | async-done | bytes 917520 | tf_op jit(solution)/shard_map/psum | solution.py:75
  195.3 1.4 multiply_reduce_fusion
  196.7 5.2 convolution_convert_fusion
  201.9 7.4 %all-to-all-start.2 = ((bf16[32,16,7168]{2,1,0:T(8,128)(2,1)}), bf16[32,16,7168]{2,1,0:T(8,128)(2,1)}, u32[]{:S(2)}, u32[]{:S(2)}) async-start(bf16[32,16,7168]{2,1,0:T(8,128)(2,1)} %bitcast.59), calls=%async_computation.2 | async-start | bytes 14680064 | tf_op jit(solution)/shard_map/all_to_all | solution.py:96
  209.3 7.3 %copy.36 = bf16[896,8,2,256]{3,1,2,0:T(8,128)(2,1)} copy(bf16[896,8,2,256]{3,2,1,0:T(2,128)(2,1)} %bitcast.60) | data formatting | bytes 14680064
  216.6 84.9 %all-to-all-done.2 = bf16[32,16,7168]{2,1,0:T(8,128)(2,1)} async-done(((bf16[32,16,7168]{2,1,0:T(8,128)(2,1)}), bf16[32,16,7168]{2,1,0:T(8,128)(2,1)}, u32[]{:S(2)}, u32[]{:S(2)}) %all-to-all-start.2) | async-done | bytes 7340064 | tf_op jit(solution)/shard_map/all_to_all | solution.py:96
  301.6 8.6 %fusion.31 = f32[512,512]{1,0:T(8,128)S(1)} fusion(bf16[512,7168]{1,0:T(8,128)(2,1)} %bitcast.8, bf16[7168,512]{1,0:T(8,128)(2,1)} %bitcast.61), kind=kOutput, calls=%fused_computation.63 | convolution fusion | flops 3758096384 | bytes 15728640 | tf_op jit(solution)/shard_map/dot_general | solution.py:98
  310.3 7.3 %fusion.2 = f32[32,16,7168]{2,1,0:T(8,128)} fusion(bf16[32,16,256]{2,1,0:T(8,128)(2,1)S(1)} %bitcast.63, bf16[1,256,7168]{2,1,0:T(8,128)(2,1)S(1)} %copy-done.4), kind=kOutput, calls=%fused_computation.4 | convolution fusion | flops 1879048192 | bytes 18612224 | tf_op jit(solution)/shard_map/dot_general | solution.py:102
  317.7 245.9 %reduce-scatter.2.cloned.1.call-done = f32[32,16,1792]{2,1,0:T(8,128)} async-done(((f32[32,16,7168]{2,1,0:T(8,128)}), f32[32,16,1792]{2,1,0:T(8,128)}) %reduce-scatter.2.cloned.1.call-update) | async-done | bytes 3670032 | tf_op jit(solution)/shard_map/reduce_scatter | solution.py:104
  563.5 7.4 %all-to-all-start.3 = ((f32[32,16,1792]{2,1,0:T(8,128)}), f32[32,16,1792]{2,1,0:T(8,128)}, u32[]{:S(2)}, u32[]{:S(2)}) async-start(f32[32,16,1792]{2,1,0:T(8,128)} %reduce-scatter.2.cloned.1.call-done), calls=%async_computation.4 | async-start | bytes 7340032 | tf_op jit(solution)/shard_map/all_to_all | solution.py:105
  572.0 46.6 %all-to-all-done.3 = f32[32,16,1792]{2,1,0:T(8,128)} async-done(((f32[32,16,1792]{2,1,0:T(8,128)}), f32[32,16,1792]{2,1,0:T(8,128)}, u32[]{:S(2)}, u32[]{:S(2)}) %all-to-all-start.3) | async-done | bytes 3670048 | tf_op jit(solution)/shard_map/all_to_all | solution.py:105
  618.6 5.5 gather_fusion
  624.1 2.1 fusion.4
  (48 shorter events, 5.2 us)
Async XLA Ops:
  6.5 119.2 %copy-start = (bf16[4096,224]{0,1:T(8,128)(2,1)S(1)}, bf16[4096,224]{0,1:T(8,128)(2,1)}, u32[]{:S(2)}) copy-start(bf16[4096,224]{0,1:T(8,128)(2,1)} %param.18) | copy-start | bytes 5505028
  6.5 188.8 %all-reduce.2.cloned.1.call-start = ((), (), s32[]{:S(2)}) async-start(), calls=%async_computation.5 | async-start | bytes 1835008 | tf_op jit(solution)/shard_map/psum | solution.py:75
  10.0 7.2 %copy-start.2 = (bf16[32,192,576]{2,1,0:T(8,128)(2,1)S(1)}, bf16[32,192,576]{2,1,0:T(8,128)(2,1)}, u32[]{:S(2)}) copy-start(bf16[32,192,576]{2,1,0:T(8,128)(2,1)} %param.14) | copy-start | bytes 21233668
  17.2 2.2 copy-start.3
  128.1 24.3 %copy-start.8 = (s32[32,8]{0,1:T(8,128)S(1)}, s32[32,8]{0,1:T(8,128)}, u32[]{:S(2)}) copy-start(s32[32,8]{0,1:T(8,128)} %param.21) | copy-start | bytes 3076
  128.1 67.2 %copy-start.5 = (bf16[32,7168]{1,0:T(8,128)(2,1)S(1)}, bf16[32,7168]{1,0:T(8,128)(2,1)}, u32[]{:S(2)}) copy-start(bf16[32,7168]{1,0:T(8,128)(2,1)} %param.12) | copy-start | bytes 1376260
  150.2 46.5 %copy-start.7 = (f32[7168]{0:T(1024)S(1)}, f32[7168]{0:T(1024)}, u32[]{:S(2)}) copy-start(f32[7168]{0:T(1024)} %param.19) | copy-start | bytes 86020
  201.9 99.7 %all-to-all-start.2 = ((bf16[32,16,7168]{2,1,0:T(8,128)(2,1)}), bf16[32,16,7168]{2,1,0:T(8,128)(2,1)}, u32[]{:S(2)}, u32[]{:S(2)}) async-start(bf16[32,16,7168]{2,1,0:T(8,128)(2,1)} %bitcast.59), calls=%async_computation.2 | async-start | bytes 14680064 | tf_op jit(solution)/shard_map/all_to_all | solution.py:96
  209.3 354.3 %reduce-scatter.2.cloned.1.call-start = ((), (), s32[]{:S(2)}) async-start(), calls=%async_computation.6 | async-start | bytes 18350080 | tf_op jit(solution)/shard_map/reduce_scatter | solution.py:104
  301.6 8.8 %copy-start.4 = (bf16[1,256,7168]{2,1,0:T(8,128)(2,1)S(1)}, bf16[1,256,7168]{2,1,0:T(8,128)(2,1)}, u32[]{:S(2)}) copy-start(bf16[1,256,7168]{2,1,0:T(8,128)(2,1)} %param.23) | copy-start | bytes 11010052
  317.7 253.4 %copy-start.6 = (bf16[7168,32]{0,1:T(8,128)(2,1)S(1)}, bf16[7168,32]{0,1:T(8,128)(2,1)}, u32[]{:S(2)}) copy-start(bf16[7168,32]{0,1:T(8,128)(2,1)} %param.20) | copy-start | bytes 1376260
  563.5 55.1 %all-to-all-start.3 = ((f32[32,16,1792]{2,1,0:T(8,128)}), f32[32,16,1792]{2,1,0:T(8,128)}, u32[]{:S(2)}, u32[]{:S(2)}) async-start(f32[32,16,1792]{2,1,0:T(8,128)} %reduce-scatter.2.cloned.1.call-done), calls=%async_computation.4 | async-start | bytes 7340032 | tf_op jit(solution)/shard_map/all_to_all | solution.py:105
  618.6 8.3 %copy-start.1 = (bf16[4096,224]{0,1:T(8,128)(2,1)S(1)}, bf16[4096,224]{0,1:T(8,128)(2,1)}, u32[]{:S(2)}) copy-start(bf16[4096,224]{0,1:T(8,128)(2,1)} %param.18) | copy-start | bytes 5505028
Sparse Core Ops, SparseCore 0:
  152.5 42.7 all-reduce.1
  317.8 245.7 reduce-scatter.1
